TPU v7x, 32 devices: a whole 2x2x4 slice. The times are simulated.
32 devices in a mesh: section: 8 (over z, core), tensor: 4 (over y, x).
Axes of the slice: x: 2, y: 2, z: 4, core: 2. Of those that a mesh axis runs over, the one named last changes fastest.
Arguments:
- fwd_in: bfloat16 [8, 128, 2304], P('section', None, 'tensor'), may hold values from -6 to 6
- back_in: bfloat16 [8, 128, 2304], P('section', None, 'tensor'), may hold values from -0.59765625 to 0.59765625
- stash: bfloat16 [2, 8, 128, 2304], P(None, 'section', None, 'tensor'), may hold values from -6 to 6
- w_qkv: bfloat16 [8, 2304, 3, 4, 128], P('section', None, None, 'tensor'), may hold values from -0.125 to 0.125
- w_out: bfloat16 [8, 4, 128, 2304], P('section', 'tensor'), may hold values from -0.25 to 0.25
- norm_gain: bfloat16 [8, 2304], P('section'), may hold values from 0.25 to 1.75
- final_gain: bfloat16 [2304], replicated, may hold values from 0.25 to 1.75
- table: bfloat16 [8192, 2304], P(('section', 'tensor')), may hold values from -0.5625 to 0.5625
- ids: int32 [2, 128], replicated, may hold values from 0 to 8191
- back_ids: int32 [2, 128], replicated, may hold values from 0 to 8191
- targets: int32 [2, 128], replicated, may hold values from 0 to 8191
Outputs:
- fwd_out: bfloat16 [8, 128, 2304], P('section', None, 'tensor')
- back_out: bfloat16 [8, 128, 2304], P('section', None, 'tensor')
- table_grad: bfloat16 [8192, 2304], P(('section', 'tensor'))
- losses: float32 [2], replicated
All inputs are finite; a program needn't handle non-finite values.
Results may differ from a plain program's by a relative error of at most 0.035.
Values may be sent and summed in bfloat16 or wider, within the bound.
No kernel may reach another device: no remote copies, remote signals or barrier semaphores. Data moves between devices by JAX's collectives and lax.ppermute only.
A program may use at most 64 MiB of HBM per device.

v0:
```python
import math
import jax
import jax.numpy as jnp
from jax import lax
from jax.sharding import PartitionSpec as P

EPS = 1e-06
ATTN_CAP = 50.0
LOGIT_CAP = 30.0


def for_sending(x):

    def short(part):
        return part.astype(jnp.bfloat16) if part.dtype == jnp.float32 else part

    return jax.tree.map(short, x)


def passed_along(block, axis, distance):
    devices = range(lax.axis_size(axis))
    route = [(i - distance, i) for i in devices if i - distance in devices]
    return lax.ppermute(block, axis, route)


def broadcast(block, axis, holder):
    block = jnp.where(lax.axis_index(axis) == holder, block, jnp.zeros_like(block))
    return lax.psum(block, axis)


def widen(values):
    return jax.tree.map(
        lambda part, own: part.astype(own.dtype),
        lax.all_gather(for_sending(values), "tensor", axis=1, tiled=True),
        values,
    )


def sum_width(term):
    return lax.psum_scatter(
        term.astype(jnp.bfloat16), "tensor", scatter_dimension=1, tiled=True
    ).astype(jnp.float32)


def stat_width(values):
    return lax.psum(values, "tensor")


def sum_section(values):
    return jax.tree.map(
        lambda part: part.astype(jnp.float32), lax.psum(for_sending(values), "section")
    )


def pass_section(values, offset):
    return passed_along(values, "section", offset)


def feed(values, root):
    return broadcast(widen(values), "section", root)


def reduce_lookup(parts, width_pos, piece):
    summed = lax.psum(parts, ("section", "tensor"))
    return lax.dynamic_slice_in_dim(summed, width_pos * piece, piece, 1)


def row_scale(values):
    return lax.rsqrt(jnp.mean(values * values, axis=-1, keepdims=True) + EPS)


def attend(normed, weights):
    qkv = jnp.einsum("rd,dchk->chrk", normed, weights, preferred_element_type=jnp.float32).astype(
        jnp.bfloat16
    )
    query, keys, values = (qkv[0], qkv[1], qkv[2])
    length = normed.shape[0]
    scores = jnp.einsum(
        "hqk,hsk->hqs", query, keys, preferred_element_type=jnp.float32
    ) * query.shape[-1] ** (-0.5)
    capped = jnp.tanh(scores / ATTN_CAP)
    places = lax.iota(jnp.int32, length)
    causal = places[None, :] <= places[:, None]
    raised = jnp.where(causal[None], jnp.exp(ATTN_CAP * capped), 0.0)
    probs = (raised / jnp.sum(raised, axis=-1, keepdims=True)).astype(jnp.bfloat16)
    mixed = jnp.einsum("hqs,hsk->hqk", probs, values, preferred_element_type=jnp.float32).astype(
        jnp.bfloat16
    )
    return (query, keys, values, capped, probs, mixed)


def norm_back(xfull, xpiece, gpiece, dnorm, full_width):
    scale = row_scale(xfull)
    stat = stat_width(jnp.sum(xpiece * gpiece * dnorm, axis=1))
    return scale * gpiece * dnorm - xpiece * scale**3 * stat[:, None] / full_width


def body(
    fwd_in, back_in, stash, w_qkv, w_out, norm_gain, final_gain, table, ids, back_ids, targets
):
    section_pos = lax.axis_index("section")
    section_count = lax.axis_size("section")
    width_pos = lax.axis_index("tensor")
    width_count = lax.axis_size("tensor")
    acts = fwd_in[0]
    cots = back_in[0]
    rows, piece = acts.shape
    full_width = piece * width_count
    vocab_rows = table.shape[0]
    first_col = (section_pos * width_count + width_pos) * vocab_rows
    columns = first_col + lax.iota(jnp.int32, vocab_rows)
    emb_scale = math.sqrt(full_width)
    gain = norm_gain[0].astype(jnp.float32)
    gain_piece = lax.dynamic_slice_in_dim(gain, width_pos * piece, piece, 0)
    fgain = final_gain.astype(jnp.float32)
    fgain_piece = lax.dynamic_slice_in_dim(fgain, width_pos * piece, piece, 0)
    weights = w_qkv[0]
    outw = w_out[0]
    ticks = ids.shape[0]
    is_first = section_pos == 0
    is_last = section_pos == section_count - 1
    grad = jnp.zeros((vocab_rows, full_width), jnp.float32)
    losses = []
    previous = acts
    for tick in range(ticks):
        xfull = widen(acts).astype(jnp.float32)
        normed = (xfull * row_scale(xfull) * gain).astype(jnp.bfloat16)
        mixed = attend(normed, weights)[5]
        part = jnp.einsum("hrk,hkd->rd", mixed, outw, preferred_element_type=jnp.float32)
        outs_fwd = (acts.astype(jnp.float32) + sum_width(part)).astype(jnp.bfloat16)
        hidden = feed(outs_fwd, section_count - 1).astype(jnp.float32)
        hscale = row_scale(hidden)
        hnormed = (hidden * hscale * fgain).astype(jnp.bfloat16)
        raw = lax.dot_general(
            hnormed, table, (((1,), (1,)), ((), ())), preferred_element_type=jnp.float32
        )
        capped = jnp.tanh(raw / LOGIT_CAP)
        logits = LOGIT_CAP * capped
        raised = jnp.exp(logits)
        hit = targets[tick][:, None] == columns[None, :]
        tile_sums = stat_width(
            (jnp.sum(raised, axis=1), jnp.sum(jnp.where(hit, logits, 0.0), axis=1))
        )
        total, picked = sum_section(tile_sums)
        losses.append(jnp.mean(jnp.log(total) - picked))
        dlog = (
            (raised / total[:, None] - hit.astype(jnp.float32)) * (1.0 - capped * capped)
        ).astype(jnp.bfloat16)
        dpart = jnp.dot(dlog, table, preferred_element_type=jnp.float32)
        dhid = sum_section(sum_width(dpart))
        grad = grad + lax.dot_general(
            dlog, hnormed, (((0,), (0,)), ((), ())), preferred_element_type=jnp.float32
        )
        hpiece = lax.dynamic_slice_in_dim(hidden, width_pos * piece, piece, 1)
        cot_last = norm_back(hidden, hpiece, fgain_piece, dhid, full_width).astype(jnp.bfloat16)
        inputs_back = stash[tick, 0]
        if tick > 0:
            inputs_back = jnp.where(is_last, previous, inputs_back)
        bfull, upper = widen((inputs_back, cots))
        bfloat = bfull.astype(jnp.float32)
        bnormed = (bfloat * row_scale(bfloat) * gain).astype(jnp.bfloat16)
        query, keys, values, acapped, probs, amixed = attend(bnormed, weights)
        dmix = jnp.einsum("rd,hkd->hrk", upper, outw, preferred_element_type=jnp.float32).astype(
            jnp.bfloat16
        )
        dprob = jnp.einsum("hrk,hsk->hrs", dmix, values, preferred_element_type=jnp.float32)
        pfull = probs.astype(jnp.float32)
        dscore = pfull * (dprob - jnp.sum(dprob * pfull, axis=-1, keepdims=True))
        dlogit = (dscore * (1.0 - acapped * acapped) * query.shape[-1] ** (-0.5)).astype(
            jnp.bfloat16
        )
        dquery = jnp.einsum(
            "hqs,hsk->hqk", dlogit, keys, preferred_element_type=jnp.float32
        ).astype(jnp.bfloat16)
        dkeys = jnp.einsum(
            "hqs,hqk->hsk", dlogit, query, preferred_element_type=jnp.float32
        ).astype(jnp.bfloat16)
        dvalues = jnp.einsum(
            "hqs,hqk->hsk", probs, dmix, preferred_element_type=jnp.float32
        ).astype(jnp.bfloat16)
        stacked = jnp.stack([dquery, dkeys, dvalues])
        dterm = jnp.einsum("chrk,dchk->rd", stacked, weights, preferred_element_type=jnp.float32)
        dnorm = sum_width(dterm)
        bpiece = lax.dynamic_slice_in_dim(bfloat, width_pos * piece, piece, 1)
        dxf = norm_back(bfloat, bpiece, gain_piece, dnorm, full_width)
        outs_back = (cots.astype(jnp.float32) + dxf).astype(jnp.bfloat16)
        leaving = feed(outs_back, 0)
        back_hits = (back_ids[tick][:, None] == columns[None, :]).astype(jnp.bfloat16)
        look_grad = lax.dot_general(
            back_hits, leaving, (((0,), (0,)), ((), ())), preferred_element_type=jnp.float32
        )
        grad = grad + look_grad * emb_scale
        hits = (ids[tick][:, None] == columns[None, :]).astype(jnp.bfloat16)
        embedded = reduce_lookup(
            jnp.dot(hits, table, preferred_element_type=jnp.float32), width_pos, piece
        )
        entering = (embedded * emb_scale).astype(jnp.bfloat16)
        previous = acts
        acts = jnp.where(is_first, entering, pass_section(outs_fwd, 1))
        cots = jnp.where(is_last, cot_last, pass_section(outs_back, -1))
    return (acts[None], cots[None], grad.astype(jnp.bfloat16), jnp.stack(losses))


def solution(mesh):
    return jax.shard_map(
        body,
        mesh=mesh,
        in_specs=(
            P("section", None, "tensor"),
            P("section", None, "tensor"),
            P(None, "section", None, "tensor"),
            P("section", None, None, "tensor", None),
            P("section", "tensor", None, None),
            P("section", None),
            P(),
            P(("section", "tensor"), None),
            P(),
            P(),
            P(),
        ),
        out_specs=(
            P("section", None, "tensor"),
            P("section", None, "tensor"),
            P(("section", "tensor"), None),
            P(),
        ),
        check_vma=False,
    )
```

profile of v0, /device:TPU:0, one launch (start us, length us, event | category | flops | bytes accessed | tf_op | source)
XLA Modules:
  0.0 578.9 jit_solution(3762362679505095675)
XLA Ops:
  8.1 12.4 %all-gather = bf16[1,128,2304]{1,2,0:T(8,128)(2,1)S(1)} all-gather(bf16[1,128,576]{1,2,0:T(8,128)(2,1)} %param.11), channel_id=2, replica_groups=mesh['section'=8,'tensor'=4] {'tensor'}, dimensions={2}, use_global_device_ids=true | all-gather | bytes 737280 | tf_op jit(solution)/shard_map/all_gather | solution.py:34
  30.5 21.3 %reduce-scatter.7.cloned.1.call-done = bf16[128,576]{0,1:T(8,128)(2,1)} async-done(((bf16[128,2304]{0,1:T(8,128)(2,1)}), bf16[128,576]{0,1:T(8,128)(2,1)}) %reduce-scatter.7.cloned.1.call-update) | async-done | bytes 147472 | tf_op jit(solution)/shard_map/reduce_scatter | solution.py:40
  55.8 113.7 %all-reduce.14.cloned.1.call-done = (f32[128,2304]{0,1:T(8,128)}, f32[128,2304]{0,1:T(8,128)}) async-done(((f32[128,2304]{0,1:T(8,128)}, f32[128,2304]{0,1:T(8,128)}), (f32[128,2304]{0,1:T(8,128)}, f32[128,2304]{0,1:T(8,128)})) %all-reduce.14.cloned.1.call-update) | async-done | bytes 2359312 | tf_op jit(solution)/shard_map/psum | solution.py:64
  171.2 11.3 %all_gather.31 = bf16[128,2304]{0,1:T(8,128)(2,1)S(1)} all-gather(bf16[128,576]{0,1:T(8,128)(2,1)S(1)} %fusion.112), channel_id=1, replica_groups=mesh['section'=8,'tensor'=4] {'tensor'}, dimensions={1}, use_global_device_ids=true | all-gather | bytes 737280 | tf_op jit(solution)/shard_map/all_gather | solution.py:34
  188.2 10.5 %all_gather.33 = bf16[128,2304]{0,1:T(8,128)(2,1)S(1)} all-gather(bf16[128,576]{0,1:T(8,128)(2,1)} %add_convert_fusion.1), channel_id=1, replica_groups=mesh['section'=8,'tensor'=4] {'tensor'}, dimensions={1}, use_global_device_ids=true | all-gather | bytes 737280 | tf_op jit(solution)/shard_map/all_gather | solution.py:34
  199.5 13.0 %reduce-scatter.9.cloned.1.call-done = bf16[128,576]{0,1:T(8,128)(2,1)} async-done(((bf16[128,2304]{0,1:T(8,128)(2,1)}), bf16[128,576]{0,1:T(8,128)(2,1)}) %reduce-scatter.9.cloned.1.call-update) | async-done | bytes 147472 | tf_op jit(solution)/shard_map/reduce_scatter | solution.py:40
  214.2 10.2 %all_gather.32 = bf16[128,2304]{0,1:T(8,128)(2,1)S(1)} all-gather(bf16[128,576]{0,1:T(8,128)(2,1)S(1)} %add_convert_fusion), channel_id=1, replica_groups=mesh['section'=8,'tensor'=4] {'tensor'}, dimensions={1}, use_global_device_ids=true | all-gather | bytes 737280 | tf_op jit(solution)/shard_map/all_gather | solution.py:34
  228.3 11.7 %all-gather.2 = bf16[1,128,2304]{1,2,0:T(8,128)(2,1)} all-gather(bf16[1,128,576]{1,2,0:T(8,128)(2,1)} %param.12), channel_id=4, replica_groups=mesh['section'=8,'tensor'=4] {'tensor'}, dimensions={2}, use_global_device_ids=true | all-gather | bytes 737280 | tf_op jit(solution)/shard_map/all_gather | solution.py:34
  241.2 43.7 %all-reduce.20.cloned.1.call-done = (bf16[128,2304]{0,1:T(8,128)(2,1)}, bf16[128,2304]{0,1:T(8,128)(2,1)}) async-done(((bf16[128,2304]{0,1:T(8,128)(2,1)}, bf16[128,2304]{0,1:T(8,128)(2,1)}), (bf16[128,2304]{0,1:T(8,128)(2,1)}, bf16[128,2304]{0,1:T(8,128)(2,1)})) %all-reduce.20.cloned.1.call-update) | async-done | bytes 1179664 | tf_op jit(solution)/shard_map/psum | solution.py:28
  291.1 10.7 %all-reduce.3 = (bf16[128]{0:T(256)(128)(2,1)}, bf16[128]{0:T(256)(128)(2,1)}) all-reduce(f32[128]{0:T(128)} %get-tuple-element.5, f32[128]{0:T(128)} %get-tuple-element.10), channel_id=1, replica_groups=mesh['section'=8,'tensor'=4] {'tensor'}, use_global_device_ids=true, to_apply=%region_20.21 | all-reduce | flops 256 | bytes 1536 | tf_op jit(solution)/shard_map/psum | solution.py:46
  301.8 14.3 %all-reduce.5 = (bf16[128]{0:T(256)(128)(2,1)}, bf16[128]{0:T(256)(128)(2,1)}) all-reduce(bf16[128]{0:T(256)(128)(2,1)} %get-tuple-element.21, bf16[128]{0:T(256)(128)(2,1)} %get-tuple-element.20), channel_id=1, replica_groups=mesh['section'=8,'tensor'=4] {'section'}, use_global_device_ids=true, to_apply=%region_12.13 | all-reduce | flops 256 | bytes 1024 | tf_op jit(solution)/shard_map/psum | solution.py:51
  319.8 12.8 %all-gather.1 = bf16[1,1,128,2304]{2,3,1,0:T(8,128)(2,1)S(1)} all-gather(bf16[1,1,128,576]{2,3,1,0:T(8,128)(2,1)} %slice.70), channel_id=3, replica_groups=mesh['section'=8,'tensor'=4] {'tensor'}, dimensions={3}, use_global_device_ids=true | all-gather | bytes 737280 | tf_op jit(solution)/shard_map/all_gather | solution.py:34
  342.8 10.7 %all_gather.36 = bf16[128,2304]{0,1:T(8,128)(2,1)S(1)} all-gather(bf16[128,576]{0,1:T(8,128)(2,1)S(1)} %bitcast_select_fusion), channel_id=1, replica_groups=mesh['section'=8,'tensor'=4] {'tensor'}, dimensions={1}, use_global_device_ids=true | all-gather | bytes 737280 | tf_op jit(solution)/shard_map/all_gather | solution.py:34
  356.7 13.5 %reduce-scatter.13.cloned.1.call-done = bf16[128,576]{0,1:T(8,128)(2,1)} async-done(((bf16[128,2304]{0,1:T(8,128)(2,1)}), bf16[128,576]{0,1:T(8,128)(2,1)}) %reduce-scatter.13.cloned.1.call-update) | async-done | bytes 147472 | tf_op jit(solution)/shard_map/reduce_scatter | solution.py:40
  375.4 22.8 %reduce-scatter.15.cloned.1.call-done = bf16[128,576]{0,1:T(8,128)(2,1)} async-done(((bf16[128,2304]{0,1:T(8,128)(2,1)}), bf16[128,576]{0,1:T(8,128)(2,1)}) %reduce-scatter.15.cloned.1.call-update) | async-done | bytes 147472 | tf_op jit(solution)/shard_map/reduce_scatter | solution.py:40
  402.2 21.0 %all-reduce.18.cloned.1.call-done = (bf16[128,576]{0,1:T(8,128)(2,1)}, bf16[128,576]{0,1:T(8,128)(2,1)}) async-done(((bf16[128,576]{0,1:T(8,128)(2,1)}, bf16[128,576]{0,1:T(8,128)(2,1)}), (bf16[128,576]{0,1:T(8,128)(2,1)}, bf16[128,576]{0,1:T(8,128)(2,1)})) %all-reduce.18.cloned.1.call-update) | async-done | bytes 294928 | tf_op jit(solution)/shard_map/psum | solution.py:51
  425.2 10.5 %all-reduce.2 = (f32[128]{0:T(128)}, f32[128]{0:T(128)}) all-reduce(f32[128]{0:T(128)} %fusion.101, f32[128]{0:T(128)} %get-tuple-element.9), channel_id=1, replica_groups=mesh['section'=8,'tensor'=4] {'tensor'}, use_global_device_ids=true, to_apply=%region_31.32 | all-reduce | flops 256 | bytes 2048 | tf_op jit(solution)/shard_map/psum | solution.py:46
  444.5 11.0 %all_gather.37 = bf16[128,2304]{0,1:T(8,128)(2,1)S(1)} all-gather(bf16[128,576]{0,1:T(8,128)(2,1)S(1)} %fusion.113), channel_id=1, replica_groups=mesh['section'=8,'tensor'=4] {'tensor'}, dimensions={1}, use_global_device_ids=true | all-gather | bytes 737280 | tf_op jit(solution)/shard_map/all_gather | solution.py:34
  462.3 13.0 %all_gather.38 = bf16[128,2304]{0,1:T(8,128)(2,1)S(1)} all-gather(bf16[128,576]{0,1:T(8,128)(2,1)S(1)} %copy-done.18), channel_id=1, replica_groups=mesh['section'=8,'tensor'=4] {'tensor'}, dimensions={1}, use_global_device_ids=true | all-gather | bytes 737280 | tf_op jit(solution)/shard_map/all_gather | solution.py:34
  476.2 7.2 %reduce-scatter.17.cloned.1.call-done = bf16[128,576]{0,1:T(8,128)(2,1)} async-done(((bf16[128,2304]{0,1:T(8,128)(2,1)}), bf16[128,576]{0,1:T(8,128)(2,1)}) %reduce-scatter.17.cloned.1.call-update) | async-done | bytes 147472 | tf_op jit(solution)/shard_map/reduce_scatter | solution.py:40
  484.6 9.3 %all-reduce.1 = (f32[128]{0:T(128)S(1)}, f32[128]{0:T(128)S(1)}, bf16[128]{0:T(256)(128)(2,1)S(1)}, bf16[128]{0:T(256)(128)(2,1)S(1)}) all-reduce(f32[128]{0:T(128)S(1)} %fusion.105, f32[128]{0:T(128)S(1)} %copy-done.55, f32[128]{0:T(128)S(1)} %copy-done.63, f32[128]{0:T(128)S(1)} %copy-done.62), channel_id=1, replica_groups=mesh['section'=8,'tensor'=4] {'tensor'}, use_global_device_ids=true, to_apply=%region_37.38 | all-reduce | flops 512 | bytes 3584 | tf_op jit(solution)/shard_map/psum | solution.py:46
  495.1 10.6 %all_gather.39 = bf16[128,2304]{0,1:T(8,128)(2,1)S(1)} all-gather(bf16[128,576]{0,1:T(8,128)(2,1)S(1)} %fusion.104), channel_id=1, replica_groups=mesh['section'=8,'tensor'=4] {'tensor'}, dimensions={1}, use_global_device_ids=true | all-gather | bytes 737280 | tf_op jit(solution)/shard_map/all_gather | solution.py:34
  510.3 17.9 %all-reduce.4 = (bf16[128]{0:T(256)(128)(2,1)S(1)}, bf16[128]{0:T(256)(128)(2,1)S(1)}) all-reduce(bf16[128]{0:T(256)(128)(2,1)S(1)} %get-tuple-element.16, bf16[128]{0:T(256)(128)(2,1)S(1)} %get-tuple-element.17), channel_id=1, replica_groups=mesh['section'=8,'tensor'=4] {'section'}, use_global_device_ids=true, to_apply=%region_46.47 | all-reduce | flops 256 | bytes 1024 | tf_op jit(solution)/shard_map/psum | solution.py:51
  533.0 33.5 %all-reduce.16.cloned.1.call-done = (bf16[128,2304]{0,1:T(8,128)(2,1)}, bf16[128,2304]{0,1:T(8,128)(2,1)}) async-done(((bf16[128,2304]{0,1:T(8,128)(2,1)}, bf16[128,2304]{0,1:T(8,128)(2,1)}), (bf16[128,2304]{0,1:T(8,128)(2,1)}, bf16[128,2304]{0,1:T(8,128)(2,1)})) %all-reduce.16.cloned.1.call-update) | async-done | bytes 1179664 | tf_op jit(solution)/shard_map/psum | solution.py:28
  (245 shorter events, 94.5 us)
Async XLA Ops:
  8.0 43.8 %reduce-scatter.7.cloned.1.call-start = ((), (), s32[]{:S(2)}) async-start(), calls=%async_computation.6 | async-start | bytes 737280 | tf_op jit(solution)/shard_map/reduce_scatter | solution.py:40
  26.3 143.2 %all-reduce.14.cloned.1.call-start = ((), (), s32[]{:S(2)}) async-start(), calls=%async_computation.12 | async-start | bytes 4718592 | tf_op jit(solution)/shard_map/psum | solution.py:64
  26.4 310.4 %copy-start.30 = (s32[256]{0:T(256)}, s32[256]{0:T(256)S(1)}, u32[]{:S(2)}) copy-start(s32[256]{0:T(256)S(1)} %iota_add_fusion) | copy-start | bytes 3076
  30.5 182.1 %reduce-scatter.9.cloned.1.call-start = ((), (), s32[]{:S(2)}) async-start(), calls=%async_computation.7 | async-start | bytes 737280 | tf_op jit(solution)/shard_map/reduce_scatter | solution.py:40
  53.5 116.0 %collective-permute-start = (bf16[128,576]{0,1:T(8,128)(2,1)}, bf16[128,576]{0,1:T(8,128)(2,1)}, u32[]{:S(2)}, u32[]{:S(2)}) collective-permute-start(bf16[128,576]{0,1:T(8,128)(2,1)} %add_convert_fusion.1), channel_id=1, source_target_pairs={{0,4},{4,8},{8,12},{12,16},{16,20},{20,24},{24,28},{1,5},{5,9},{9,... | collective-permute-start | bytes 442376 | tf_op jit(solution)/shard_map/ppermute | solution.py:23
  188.1 96.8 %all-reduce.20.cloned.1.call-start = ((), (), s32[]{:S(2)}) async-start(), calls=%async_computation.15 | async-start | bytes 2359296 | tf_op jit(solution)/shard_map/psum | solution.py:28
  225.3 131.3 %reduce-scatter.11.cloned.1.call-start = ((), (), s32[]{:S(2)}) async-start(), calls=%async_computation.8 | async-start | bytes 737280 | tf_op jit(solution)/shard_map/reduce_scatter | solution.py:40
  319.8 50.3 %reduce-scatter.13.cloned.1.call-start = ((), (), s32[]{:S(2)}) async-start(), calls=%async_computation.9 | async-start | bytes 737280 | tf_op jit(solution)/shard_map/reduce_scatter | solution.py:40
  338.7 59.5 %reduce-scatter.15.cloned.1.call-start = ((), (), s32[]{:S(2)}) async-start(), calls=%async_computation.10 | async-start | bytes 737280 | tf_op jit(solution)/shard_map/reduce_scatter | solution.py:40
  342.7 80.5 %all-reduce.18.cloned.1.call-start = ((), (), s32[]{:S(2)}) async-start(), calls=%async_computation.14 | async-start | bytes 589824 | tf_op jit(solution)/shard_map/psum | solution.py:51
  370.2 113.2 %reduce-scatter.17.cloned.1.call-start = ((), (), s32[]{:S(2)}) async-start(), calls=%async_computation.11 | async-start | bytes 737280 | tf_op jit(solution)/shard_map/reduce_scatter | solution.py:40
  373.3 26.6 %copy-start.8 = (bf16[128,2304]{0,1:T(8,128)(2,1)S(1)}, bf16[128,2304]{0,1:T(8,128)(2,1)}, u32[]{:S(2)}) copy-start(bf16[128,2304]{0,1:T(8,128)(2,1)} %get-tuple-element.30) | copy-start | bytes 1769476
  374.2 69.0 %copy-start.33 = (f32[576]{0:T(1024)}, f32[576]{0:T(1024)S(1)}, u32[]{:S(2)}) copy-start(f32[576]{0:T(1024)S(1)} %dynamic_slice.28) | copy-start | bytes 6916
  375.3 25.8 %copy-start.6 = (bf16[128,2304]{0,1:T(8,128)(2,1)S(1)}, bf16[128,2304]{0,1:T(8,128)(2,1)}, u32[]{:S(2)}) copy-start(bf16[128,2304]{0,1:T(8,128)(2,1)} %get-tuple-element.31) | copy-start | bytes 1769476
  401.1 34.5 %copy-start.59 = (f32[128]{0:T(128)S(1)}, f32[128]{0:T(128)}, u32[]{:S(2)}) copy-start(f32[128]{0:T(128)} %copy-done.58) | copy-start | bytes 1540
  402.2 41.0 %copy-start.47 = (f32[128]{0:T(128)S(1)}, f32[128]{0:T(128)}, u32[]{:S(2)}) copy-start(f32[128]{0:T(128)} %copy-done.46) | copy-start | bytes 1540
  436.9 6.3 %collective-permute-start.2 = (bf16[128,576]{0,1:T(8,128)(2,1)S(1)}, bf16[128,576]{0,1:T(8,128)(2,1)S(1)}, u32[]{:S(2)}, u32[]{:S(2)}) collective-permute-start(bf16[128,576]{0,1:T(8,128)(2,1)S(1)} %fusion.100), channel_id=1, source_target_pairs={{4,0},{8,4},{12,8},{16,12},{20,16},{24,20},{28,24},{5,1},{9,5},{13... | collective-permute-start | bytes 442376 | tf_op jit(solution)/shard_map/ppermute | solution.py:23
  439.5 18.7 %collective-permute-start.1 = (bf16[128,576]{0,1:T(8,128)(2,1)}, bf16[128,576]{0,1:T(8,128)(2,1)}, u32[]{:S(2)}, u32[]{:S(2)}) collective-permute-start(bf16[128,576]{0,1:T(8,128)(2,1)} %copy-done.15), channel_id=1, source_target_pairs={{0,4},{4,8},{8,12},{12,16},{16,20},{20,24},{24,28},{1,5},{5,9},{9,... | collective-permute-start | bytes 442376 | tf_op jit(solution)/shard_map/ppermute | solution.py:23
  458.1 108.4 %all-reduce.16.cloned.1.call-start = ((), (), s32[]{:S(2)}) async-start(), calls=%async_computation.13 | async-start | bytes 2359296 | tf_op jit(solution)/shard_map/psum | solution.py:28
  462.2 31.6 %copy-start.12 = (bf16[128,576]{0,1:T(8,128)(2,1)S(1)}, bf16[128,576]{0,1:T(8,128)(2,1)}, u32[]{:S(2)}) copy-start(bf16[128,576]{0,1:T(8,128)(2,1)} %copy-done.11) | copy-start | bytes 442372
  462.2 31.6 %copy-start.57 = (f32[128]{0:T(128)S(1)}, f32[128]{0:T(128)}, u32[]{:S(2)}) copy-start(f32[128]{0:T(128)} %copy-done.56) | copy-start | bytes 1540
  462.3 31.6 %copy-start.64 = (f32[128]{0:T(128)S(1)}, f32[128]{0:T(128)}, u32[]{:S(2)}) copy-start(f32[128]{0:T(128)} %get-tuple-element.40) | copy-start | bytes 1540
  506.7 59.8 %copy-start.54 = (s32[128]{0:T(128)S(1)}, s32[128]{0:T(128)}, u32[]{:S(2)}) copy-start(s32[128]{0:T(128)} %get-tuple-element.33) | copy-start | bytes 1540
  509.0 22.2 %collective-permute-start.3 = (bf16[128,576]{0,1:T(8,128)(2,1)S(1)}, bf16[128,576]{0,1:T(8,128)(2,1)S(1)}, u32[]{:S(2)}, u32[]{:S(2)}) collective-permute-start(bf16[128,576]{0,1:T(8,128)(2,1)S(1)} %fusion.104), channel_id=1, source_target_pairs={{4,0},{8,4},{12,8},{16,12},{20,16},{24,20},{28,24},{5,1},{9,5},{13... | collective-permute-start | bytes 442376 | tf_op jit(solution)/shard_map/ppermute | solution.py:23
  (58 other events, 382.4 us)
Sparse Core Ops, SparseCore 0:
  26.4 25.3 reduce-scatter.6
  188.2 24.2 reduce-scatter.8
  319.9 22.2 reduce-scatter.10
  344.9 25.1 reduce-scatter.12
  373.1 25.1 reduce-scatter.14
  458.2 25.0 reduce-scatter.16
Sparse Core Ops, SparseCore 1:
  34.0 135.5 all-reduce.13
  225.4 59.5 all-reduce.19
  370.2 52.9 all-reduce.17
  506.7 59.8 all-reduce.15
where the time goes:
time: 580 us; the launch traced here: 579 us
  waiting for transfers between devices  290 us (50%)
  blocking collectives  177 us (31%)
  matrix products  41.2 us (7%)
  other arithmetic  33.3 us (6%)
  between operations  17.7 us (3%)
  local copies, waits for them, and re-layouts  10.9 us (2%)
  starting transfers between devices  8.97 us (2%)
    all_gather x10, blocking collectives, widen(): lax.all_gather(for_sending(values), 'tensor', axis=1, tiled=True)  114 us
    psum x1, waiting for transfers between devices, reduce_lookup(): summed = lax.psum(parts, ('section', 'tensor'))  114 us
    reduce_scatter x6, waiting for transfers between devices, sum_width(): lax.psum_scatter(term.astype(jnp.bfloat16), 'tensor', scatter_dimension=1...  77.8 us
    psum x2, waiting for transfers between devices, broadcast(): return lax.psum(block, axis)  77.3 us
    psum x2, blocking collectives, sum_section(): lax.psum(for_sending(values), 'section')  32.2 us
    psum x3, blocking collectives, stat_width(): return lax.psum(values, 'tensor')  30.4 us
    psum x1, waiting for transfers between devices, sum_section(): lax.psum(for_sending(values), 'section')  21 us
  transfers between devices with their start and end apart: 14, of which 9 were waited for; matrix products, arithmetic and copies ran while one was open for 8% of the time, Pallas kernels for 0%

commit v1 on v0

--- a/solution.py
+++ b/solution.py
@@ -25,7 +25,7 @@
 
 def broadcast(block, axis, holder):
     block = jnp.where(lax.axis_index(axis) == holder, block, jnp.zeros_like(block))
-    return lax.psum(block, axis)
+    return jnp.sum(lax.all_gather(block, axis), axis=0)
 
 
 def widen(values):

time: 580 us -> 695 us (1.20)
  waiting for transfers between devices: 290 us -> 344 us
  other arithmetic: 33.3 us -> 72.2 us
  local copies, waits for them, and re-layouts: 10.9 us -> 24.1 us
  blocking collectives: 177 us -> 186 us
    all_gather x0 -> x4, waiting for transfers between devices: none -> 85.6 us  [broadcast(): return jnp.sum(lax.all_gather(block, axis), axis=0)]
    psum x2 -> x0, waiting for transfers between devices: 77.3 us -> none  [broadcast(): return lax.psum(block, axis)]
    reduce_sum x0 -> x4, other arithmetic: none -> 39.4 us  [broadcast(): return jnp.sum(lax.all_gather(block, axis), axis=0)]
    psum x1, waiting for transfers between devices: 21 us -> 51.5 us  [sum_section(): lax.psum(for_sending(values), 'section')]
    unnamed x136 -> x134, local copies, waits for them, and re-layouts: 5 us -> 19.6 us
    reduce_scatter x6, waiting for transfers between devices: 77.8 us -> 91.9 us  [sum_width(): lax.psum_scatter(term.astype(jnp.bfloat16), 'tensor', scatter_dimension=1...]
    psum x2, blocking collectives: 32.2 us -> 45.2 us  [sum_section(): lax.psum(for_sending(values), 'section')]
  transfers between devices with their start and end apart: 14 -> 16, of which waited for: 9 -> 11; matrix products, arithmetic and copies ran while one was open for 8% -> 11% of each run, Pallas kernels for 0% -> 0%
where the time goes in v1:
time: 695 us; the launch traced here: 689 us
  waiting for transfers between devices  344 us (49%)
  blocking collectives  186 us (27%)
  other arithmetic  72.2 us (10%)
  matrix products  39 us (6%)
  local copies, waits for them, and re-layouts  24.1 us (3%)
  between operations  17.7 us (3%)
    psum x1, waiting for transfers between devices, reduce_lookup(): summed = lax.psum(parts, ('section', 'tensor'))  114 us
    all_gather x10, blocking collectives, widen(): lax.all_gather(for_sending(values), 'tensor', axis=1, tiled=True)  110 us
    reduce_scatter x6, waiting for transfers between devices, sum_width(): lax.psum_scatter(term.astype(jnp.bfloat16), 'tensor', scatter_dimension=1...  91.9 us
    all_gather x4, waiting for transfers between devices, broadcast(): return jnp.sum(lax.all_gather(block, axis), axis=0)  85.6 us
    psum x1, waiting for transfers between devices, sum_section(): lax.psum(for_sending(values), 'section')  51.5 us
    psum x2, blocking collectives, sum_section(): lax.psum(for_sending(values), 'section')  45.2 us
    reduce_sum x4, other arithmetic, broadcast(): return jnp.sum(lax.all_gather(block, axis), axis=0)  39.4 us
    psum x3, blocking collectives, stat_width(): return lax.psum(values, 'tensor')  30.9 us
  transfers between devices with their start and end apart: 16, of which 11 were waited for; matrix products, arithmetic and copies ran while one was open for 11% of the time, Pallas kernels for 0%

profile of v1, /device:TPU:0, one launch (start us, length us, event | category | flops | bytes accessed | tf_op | source)
XLA Modules:
  0.0 689.4 jit_solution(9370363107602811037)
XLA Ops:
  8.9 12.3 %all-gather = bf16[1,128,2304]{1,2,0:T(8,128)(2,1)S(1)} all-gather(bf16[1,128,576]{1,2,0:T(8,128)(2,1)} %param.11), channel_id=2, replica_groups=mesh['section'=8,'tensor'=4] {'tensor'}, dimensions={2}, use_global_device_ids=true | all-gather | bytes 737280 | tf_op jit(solution)/shard_map/all_gather | solution.py:34
  30.5 21.3 %reduce-scatter.7.cloned.1.call-done = bf16[128,576]{0,1:T(8,128)(2,1)} async-done(((bf16[128,2304]{0,1:T(8,128)(2,1)}), bf16[128,576]{0,1:T(8,128)(2,1)}) %reduce-scatter.7.cloned.1.call-update) | async-done | bytes 147472 | tf_op jit(solution)/shard_map/reduce_scatter | solution.py:40
  55.7 113.8 %all-reduce.10.cloned.1.call-done = (f32[128,2304]{0,1:T(8,128)}, f32[128,2304]{0,1:T(8,128)}) async-done(((f32[128,2304]{0,1:T(8,128)}, f32[128,2304]{0,1:T(8,128)}), (f32[128,2304]{0,1:T(8,128)}, f32[128,2304]{0,1:T(8,128)})) %all-reduce.10.cloned.1.call-update) | async-done | bytes 2359312 | tf_op jit(solution)/shard_map/psum | solution.py:64
  171.2 11.3 %all_gather.55 = bf16[128,2304]{0,1:T(8,128)(2,1)S(1)} all-gather(bf16[128,576]{0,1:T(8,128)(2,1)S(1)} %fusion.112), channel_id=1, replica_groups=mesh['section'=8,'tensor'=4] {'tensor'}, dimensions={1}, use_global_device_ids=true | all-gather | bytes 737280 | tf_op jit(solution)/shard_map/all_gather | solution.py:34
  188.2 10.5 %all_gather.59 = bf16[128,2304]{0,1:T(8,128)(2,1)S(1)} all-gather(bf16[128,576]{0,1:T(8,128)(2,1)} %add_convert_fusion.1), channel_id=1, replica_groups=mesh['section'=8,'tensor'=4] {'tensor'}, dimensions={1}, use_global_device_ids=true | all-gather | bytes 737280 | tf_op jit(solution)/shard_map/all_gather | solution.py:34
  199.6 12.9 %reduce-scatter.9.cloned.1.call-done = bf16[128,576]{0,1:T(8,128)(2,1)} async-done(((bf16[128,2304]{0,1:T(8,128)(2,1)}), bf16[128,576]{0,1:T(8,128)(2,1)}) %reduce-scatter.9.cloned.1.call-update) | async-done | bytes 147472 | tf_op jit(solution)/shard_map/reduce_scatter | solution.py:40
  214.2 10.2 %all_gather.56 = bf16[128,2304]{0,1:T(8,128)(2,1)S(1)} all-gather(bf16[128,576]{0,1:T(8,128)(2,1)S(1)} %add_convert_fusion), channel_id=1, replica_groups=mesh['section'=8,'tensor'=4] {'tensor'}, dimensions={1}, use_global_device_ids=true | all-gather | bytes 737280 | tf_op jit(solution)/shard_map/all_gather | solution.py:34
  227.5 11.1 %all-gather.3 = bf16[1,1,128,2304]{2,3,1,0:T(8,128)(2,1)} all-gather(bf16[1,1,128,576]{2,3,1,0:T(8,128)(2,1)S(1)} %slice.70), channel_id=5, replica_groups=mesh['section'=8,'tensor'=4] {'tensor'}, dimensions={3}, use_global_device_ids=true | all-gather | bytes 737280 | tf_op jit(solution)/shard_map/all_gather | solution.py:34
  240.0 26.4 %all-gather.14.cloned.1.call-done = bf16[1024,2304]{0,1:T(8,128)(2,1)} async-done(((bf16[128,2304]{0,1:T(8,128)(2,1)}), bf16[1024,2304]{0,1:T(8,128)(2,1)}) %all-gather.14.cloned.1.call-update) | async-done | bytes 4718608 | tf_op jit(solution)/shard_map/all_gather | solution.py:28
  269.9 9.8 %bitcast_reduce_fusion.2 = bf16[128,2304]{0,1:T(8,128)(2,1)S(1)} fusion(bf16[288,8,8,128]{3,2,1,0:T(8,128)(2,1)S(1)} %copy.32), kind=kLoop, calls=%fused_computation.2 | loop fusion | flops 2064384 | bytes 5308416 | tf_op jit(solution)/shard_map/reduce_sum | solution.py:28
  281.4 37.4 %all-gather.12.cloned.1.call-done = bf16[1024,2304]{0,1:T(8,128)(2,1)} async-done(((bf16[128,2304]{0,1:T(8,128)(2,1)}), bf16[1024,2304]{0,1:T(8,128)(2,1)}) %all-gather.12.cloned.1.call-update) | async-done | bytes 4718608 | tf_op jit(solution)/shard_map/all_gather | solution.py:28
  336.6 10.6 %all-reduce.3 = (bf16[128]{0:T(256)(128)(2,1)}, bf16[128]{0:T(256)(128)(2,1)}) all-reduce(f32[128]{0:T(128)} %get-tuple-element.5, f32[128]{0:T(128)} %get-tuple-element.10), channel_id=1, replica_groups=mesh['section'=8,'tensor'=4] {'tensor'}, use_global_device_ids=true, to_apply=%region_20.21 | all-reduce | flops 256 | bytes 1536 | tf_op jit(solution)/shard_map/psum | solution.py:46
  347.2 14.3 %all-reduce.5 = (bf16[128]{0:T(256)(128)(2,1)}, bf16[128]{0:T(256)(128)(2,1)}) all-reduce(bf16[128]{0:T(256)(128)(2,1)} %get-tuple-element.21, bf16[128]{0:T(256)(128)(2,1)} %get-tuple-element.20), channel_id=1, replica_groups=mesh['section'=8,'tensor'=4] {'section'}, use_global_device_ids=true, to_apply=%region_12.13 | all-reduce | flops 256 | bytes 1024 | tf_op jit(solution)/shard_map/psum | solution.py:51
  365.1 13.4 %all-gather.4 = bf16[1,128,2304]{1,2,0:T(8,128)(2,1)S(1)} all-gather(bf16[1,128,576]{1,2,0:T(8,128)(2,1)} %param.12), channel_id=6, replica_groups=mesh['section'=8,'tensor'=4] {'tensor'}, dimensions={2}, use_global_device_ids=true | all-gather | bytes 737280 | tf_op jit(solution)/shard_map/all_gather | solution.py:34
  399.2 17.4 %reduce-scatter.11.cloned.1.call-done = bf16[128,576]{0,1:T(8,128)(2,1)} async-done(((bf16[128,2304]{0,1:T(8,128)(2,1)}), bf16[128,576]{0,1:T(8,128)(2,1)}) %reduce-scatter.11.cloned.1.call-update) | async-done | bytes 147472 | tf_op jit(solution)/shard_map/reduce_scatter | solution.py:40
  419.7 25.1 %reduce-scatter.15.cloned.1.call-done = bf16[128,576]{0,1:T(8,128)(2,1)} async-done(((bf16[128,2304]{0,1:T(8,128)(2,1)}), bf16[128,576]{0,1:T(8,128)(2,1)}) %reduce-scatter.15.cloned.1.call-update) | async-done | bytes 147472 | tf_op jit(solution)/shard_map/reduce_scatter | solution.py:40
  448.7 51.5 %all-reduce.12.cloned.1.call-done = (bf16[128,576]{0,1:T(8,128)(2,1)}, bf16[128,576]{0,1:T(8,128)(2,1)}) async-done(((bf16[128,576]{0,1:T(8,128)(2,1)}, bf16[128,576]{0,1:T(8,128)(2,1)}), (bf16[128,576]{0,1:T(8,128)(2,1)}, bf16[128,576]{0,1:T(8,128)(2,1)})) %all-reduce.12.cloned.1.call-update) | async-done | bytes 294928 | tf_op jit(solution)/shard_map/psum | solution.py:51
  502.2 10.5 %all-reduce.2 = (f32[128]{0:T(128)}, f32[128]{0:T(128)}) all-reduce(f32[128]{0:T(128)} %fusion.101, f32[128]{0:T(128)} %get-tuple-element.9), channel_id=1, replica_groups=mesh['section'=8,'tensor'=4] {'tensor'}, use_global_device_ids=true, to_apply=%region_31.32 | all-reduce | flops 256 | bytes 2048 | tf_op jit(solution)/shard_map/psum | solution.py:46
  518.4 10.3 %all_gather.65 = bf16[128,2304]{0,1:T(8,128)(2,1)S(1)} all-gather(bf16[128,576]{0,1:T(8,128)(2,1)S(1)} %fusion.113), channel_id=1, replica_groups=mesh['section'=8,'tensor'=4] {'tensor'}, dimensions={1}, use_global_device_ids=true | all-gather | bytes 737280 | tf_op jit(solution)/shard_map/all_gather | solution.py:34
  531.3 10.5 %all_gather.66 = bf16[128,2304]{0,1:T(8,128)(2,1)S(1)} all-gather(bf16[128,576]{0,1:T(8,128)(2,1)} %copy-done.22), channel_id=1, replica_groups=mesh['section'=8,'tensor'=4] {'tensor'}, dimensions={1}, use_global_device_ids=true | all-gather | bytes 737280 | tf_op jit(solution)/shard_map/all_gather | solution.py:34
  544.0 15.3 %reduce-scatter.17.cloned.1.call-done = bf16[128,576]{0,1:T(8,128)(2,1)} async-done(((bf16[128,2304]{0,1:T(8,128)(2,1)}), bf16[128,576]{0,1:T(8,128)(2,1)}) %reduce-scatter.17.cloned.1.call-update) | async-done | bytes 147472 | tf_op jit(solution)/shard_map/reduce_scatter | solution.py:40
  572.2 10.9 %all_gather.69 = bf16[128,2304]{0,1:T(8,128)(2,1)S(1)} all-gather(bf16[128,576]{0,1:T(8,128)(2,1)S(1)} %fusion.104), channel_id=1, replica_groups=mesh['section'=8,'tensor'=4] {'tensor'}, dimensions={1}, use_global_device_ids=true | all-gather | bytes 737280 | tf_op jit(solution)/shard_map/all_gather | solution.py:34
  594.5 30.9 %all-reduce.4 = (bf16[128]{0:T(256)(128)(2,1)S(1)}, bf16[128]{0:T(256)(128)(2,1)S(1)}) all-reduce(bf16[128]{0:T(256)(128)(2,1)S(1)} %copy-done.63, bf16[128]{0:T(256)(128)(2,1)S(1)} %copy-done.64), channel_id=1, replica_groups=mesh['section'=8,'tensor'=4] {'section'}, use_global_device_ids=true, to_apply=%region_46.47 | all-reduce | flops 256 | bytes 1024 | tf_op jit(solution)/shard_map/psum | solution.py:51
  645.2 21.9 %all-gather.18.cloned.1.call-done = bf16[1024,2304]{0,1:T(8,128)(2,1)} async-done(((bf16[128,2304]{0,1:T(8,128)(2,1)}), bf16[1024,2304]{0,1:T(8,128)(2,1)}) %all-gather.18.cloned.1.call-update) | async-done | bytes 4718608 | tf_op jit(solution)/shard_map/all_gather | solution.py:28
  (253 shorter events, 152.4 us)
Async XLA Ops:
  8.0 43.8 %reduce-scatter.7.cloned.1.call-start = ((), (), s32[]{:S(2)}) async-start(), calls=%async_computation.6 | async-start | bytes 737280 | tf_op jit(solution)/shard_map/reduce_scatter | solution.py:40
  26.3 143.2 %all-reduce.10.cloned.1.call-start = ((), (), s32[]{:S(2)}) async-start(), calls=%async_computation.16 | async-start | bytes 4718592 | tf_op jit(solution)/shard_map/psum | solution.py:64
  30.5 182.0 %reduce-scatter.9.cloned.1.call-start = ((), (), s32[]{:S(2)}) async-start(), calls=%async_computation.7 | async-start | bytes 737280 | tf_op jit(solution)/shard_map/reduce_scatter | solution.py:40
  53.5 116.0 %collective-permute-start = (bf16[128,576]{0,1:T(8,128)(2,1)}, bf16[128,576]{0,1:T(8,128)(2,1)}, u32[]{:S(2)}, u32[]{:S(2)}) collective-permute-start(bf16[128,576]{0,1:T(8,128)(2,1)} %add_convert_fusion.1), channel_id=1, source_target_pairs={{0,4},{4,8},{8,12},{12,16},{16,20},{20,24},{24,28},{1,5},{5,9},{9,... | collective-permute-start | bytes 442376 | tf_op jit(solution)/shard_map/ppermute | solution.py:23
  188.1 78.3 %all-gather.14.cloned.1.call-start = ((), (), s32[]{:S(2)}) async-start(), calls=%async_computation.13 | async-start | bytes 5308416 | tf_op jit(solution)/shard_map/all_gather | solution.py:28
  199.5 119.3 %all-gather.12.cloned.1.call-start = ((), (), s32[]{:S(2)}) async-start(), calls=%async_computation.12 | async-start | bytes 5308416 | tf_op jit(solution)/shard_map/all_gather | solution.py:28
  225.3 173.9 %reduce-scatter.13.cloned.1.call-start = ((), (), s32[]{:S(2)}) async-start(), calls=%async_computation.9 | async-start | bytes 737280 | tf_op jit(solution)/shard_map/reduce_scatter | solution.py:40
  365.0 51.5 %reduce-scatter.11.cloned.1.call-start = ((), (), s32[]{:S(2)}) async-start(), calls=%async_computation.8 | async-start | bytes 737280 | tf_op jit(solution)/shard_map/reduce_scatter | solution.py:40
  385.1 59.7 %reduce-scatter.15.cloned.1.call-start = ((), (), s32[]{:S(2)}) async-start(), calls=%async_computation.10 | async-start | bytes 737280 | tf_op jit(solution)/shard_map/reduce_scatter | solution.py:40
  389.1 111.1 %all-reduce.12.cloned.1.call-start = ((), (), s32[]{:S(2)}) async-start(), calls=%async_computation.17 | async-start | bytes 589824 | tf_op jit(solution)/shard_map/psum | solution.py:51
  416.6 142.6 %reduce-scatter.17.cloned.1.call-start = ((), (), s32[]{:S(2)}) async-start(), calls=%async_computation.11 | async-start | bytes 737280 | tf_op jit(solution)/shard_map/reduce_scatter | solution.py:40
  418.5 98.7 %copy-start.34 = (f32[576]{0:T(1024)}, f32[576]{0:T(1024)S(1)}, u32[]{:S(2)}) copy-start(f32[576]{0:T(1024)S(1)} %dynamic_slice.28) | copy-start | bytes 6916
  448.7 68.5 %copy-start.47 = (f32[128]{0:T(128)S(1)}, f32[128]{0:T(128)}, u32[]{:S(2)}) copy-start(f32[128]{0:T(128)} %get-tuple-element.39) | copy-start | bytes 1540
  513.9 3.3 collective-permute-start.2
  531.3 98.4 %all-gather.16.cloned.1.call-start = ((), (), s32[]{:S(2)}) async-start(), calls=%async_computation.14 | async-start | bytes 5308416 | tf_op jit(solution)/shard_map/all_gather | solution.py:28
  542.8 124.3 %all-gather.18.cloned.1.call-start = ((), (), s32[]{:S(2)}) async-start(), calls=%async_computation.15 | async-start | bytes 5308416 | tf_op jit(solution)/shard_map/all_gather | solution.py:28
  584.0 2.7 collective-permute-start.1
  590.8 34.6 %copy-start.61 = (bf16[128]{0:T(256)(128)(2,1)S(1)}, bf16[128]{0:T(256)(128)(2,1)}, u32[]{:S(2)}) copy-start(bf16[128]{0:T(256)(128)(2,1)} %get-tuple-element.24) | copy-start | bytes 772
  590.8 34.6 %copy-start.62 = (bf16[128]{0:T(256)(128)(2,1)S(1)}, bf16[128]{0:T(256)(128)(2,1)}, u32[]{:S(2)}) copy-start(bf16[128]{0:T(256)(128)(2,1)} %get-tuple-element.25) | copy-start | bytes 772
  590.8 37.1 %copy-start.19 = (bf16[128,576]{0,1:T(8,128)(2,1)S(1)}, bf16[128,576]{0,1:T(8,128)(2,1)}, u32[]{:S(2)}) copy-start(bf16[128,576]{0,1:T(8,128)(2,1)} %get-tuple-element.26) | copy-start | bytes 442372
  590.8 37.1 %copy-start.35 = (f32[576]{0:T(1024)S(1)}, f32[576]{0:T(1024)}, u32[]{:S(2)}) copy-start(f32[576]{0:T(1024)} %copy-done.34) | copy-start | bytes 6916
  590.8 37.1 %copy-start.58 = (f32[128]{0:T(128)S(1)}, f32[128]{0:T(128)}, u32[]{:S(2)}) copy-start(f32[128]{0:T(128)} %get-tuple-element.34) | copy-start | bytes 1540
  590.8 37.1 %copy-start.59 = (f32[128]{0:T(128)S(1)}, f32[128]{0:T(128)}, u32[]{:S(2)}) copy-start(f32[128]{0:T(128)} %get-tuple-element.15) | copy-start | bytes 1540
  593.2 34.7 %collective-permute-start.3 = (bf16[128,576]{0,1:T(8,128)(2,1)S(1)}, bf16[128,576]{0,1:T(8,128)(2,1)S(1)}, u32[]{:S(2)}, u32[]{:S(2)}) collective-permute-start(bf16[128,576]{0,1:T(8,128)(2,1)S(1)} %copy-done.21), channel_id=1, source_target_pairs={{4,0},{8,4},{12,8},{16,12},{20,16},{24,20},{28,24},{5,1},{9,5},{13... | collective-permute-start | bytes 442376 | tf_op jit(solution)/shard_map/ppermute | solution.py:23
  (57 other events, 321.4 us)
Sparse Core Ops, SparseCore 0:
  26.4 25.3 reduce-scatter.6
  188.2 24.2 reduce-scatter.8
  214.2 52.1 all-gather.13
  268.4 50.3 all-gather.11
  365.2 22.3 reduce-scatter.12
  390.9 25.6 reduce-scatter.10
  419.7 25.0 reduce-scatter.14
  447.2 52.9 all-reduce.11
  531.4 27.7 reduce-scatter.16
  560.7 53.7 all-gather.15
  616.7 50.3 all-gather.17
Sparse Core Ops, SparseCore 1:
  34.0 135.5 all-reduce.9
